TPU v7x, 256 devices: a whole 4x4x8 slice. The times are simulated.
256 devices in a mesh: slab: 64 (over z, y, core), col: 4 (over x).
Axes of the slice: x: 4, y: 4, z: 8, core: 2. Of those that a mesh axis runs over, the one named last changes fastest.
Arguments:
- recycle_basis: float32 [16, 3, 128, 8, 256], P('col', None, 'slab'), may hold values from -400 to 400
- densities: float32 [128, 8, 256], P('slab'), may hold values from 0.2 to 1
- solid_mask: int32 [128, 8, 256], P('slab'), may hold values 0 or 1
- fixed_mask: int32 [128, 8, 256], P('slab'), may hold values 0 or 1
Outputs:
- ortho_basis: float32 [16, 3, 128, 8, 256], P('col', None, 'slab')
- new_recycle: float32 [16, 3, 128, 8, 256], P('col', None, 'slab')
- r_factor: float32 [16, 16], replicated
Inputs may be any that keep to these rules, and one draw needn't show every extreme that they name: `solid_mask`: 1 marks a solid lattice voxel. `fixed_mask`: 1 marks a fixed node.
All inputs are finite; a program needn't handle non-finite values. No bound on the sum of `solid_mask` or of `fixed_mask` on one device may be relied on, other than what follows from the above.
Results may differ from a plain program's by a relative error of at most 0.0001.
Values sent between devices are 32-bit elements; how exact they have to be, the bound alone decides.
A program may use at most 64 MiB of HBM per device.

v0:
```python
import jax
import jax.numpy as jnp
import numpy as np
from jax import lax
from jax.sharding import PartitionSpec as P

void_stiffness = 0.001


def from_behind(value, axis, steps):
    count = lax.axis_size(axis)
    first, last = (max(0, -steps), min(count, count - steps))
    return lax.ppermute(value, axis, [(source, source + steps) for source in range(first, last)])


def element_matrix():
    poisson = 0.3
    lame_first = poisson / ((1.0 + poisson) * (1.0 - 2.0 * poisson))
    shear_mod = 1.0 / (2.0 * (1.0 + poisson))
    elastic = np.zeros((6, 6))
    elastic[:3, :3] = lame_first
    for k in range(3):
        elastic[k, k] = lame_first + 2.0 * shear_mod
    for k in range(3, 6):
        elastic[k, k] = shear_mod
    points = [(1.0 - 1.0 / np.sqrt(3.0)) / 2.0, (1.0 + 1.0 / np.sqrt(3.0)) / 2.0]
    matrix = np.zeros((24, 24))
    for a in points:
        for b in points:
            for d in points:
                strain = np.zeros((6, 24))
                for c in range(8):
                    ox, oy, oz = (c % 2, c // 2 % 2, c // 4)
                    weight_x = a if ox else 1.0 - a
                    weight_y = b if oy else 1.0 - b
                    weight_z = d if oz else 1.0 - d
                    slope_x = (1.0 if ox else -1.0) * weight_y * weight_z
                    slope_y = (1.0 if oy else -1.0) * weight_x * weight_z
                    slope_z = (1.0 if oz else -1.0) * weight_x * weight_y
                    strain[0, 3 * c] = slope_x
                    strain[1, 3 * c + 1] = slope_y
                    strain[2, 3 * c + 2] = slope_z
                    strain[3, 3 * c] = slope_y
                    strain[3, 3 * c + 1] = slope_x
                    strain[4, 3 * c + 1] = slope_z
                    strain[4, 3 * c + 2] = slope_y
                    strain[5, 3 * c] = slope_z
                    strain[5, 3 * c + 2] = slope_x
                matrix = matrix + strain.T @ elastic @ strain / 8.0
    return matrix.reshape(8, 3, 8, 3)


def shift_ahead(values, along):
    count = values.shape[along]
    rest = lax.slice_in_dim(values, 1, count, axis=along)
    edge = jnp.zeros_like(lax.slice_in_dim(values, 0, 1, axis=along))
    return jnp.concatenate([rest, edge], axis=along)


def shift_behind(values, along):
    count = values.shape[along]
    rest = lax.slice_in_dim(values, 0, count - 1, axis=along)
    edge = jnp.zeros_like(lax.slice_in_dim(values, 0, 1, axis=along))
    return jnp.concatenate([edge, rest], axis=along)


def element_stiffness(densities, solid_mask, start_layer, total_layers):
    full_shape = densities.shape
    depth_index = lax.broadcasted_iota(jnp.int32, full_shape, 0) + start_layer
    across_x = lax.broadcasted_iota(jnp.int32, full_shape, 1)
    across_y = lax.broadcasted_iota(jnp.int32, full_shape, 2)
    inside = (
        (depth_index < total_layers - 1)
        & (across_x < full_shape[1] - 1)
        & (across_y < full_shape[2] - 1)
    )
    values = solid_mask.astype(jnp.float32) * densities**3 + void_stiffness
    return jnp.where(inside, values, 0.0)


def element_forces(extended, stiffness, matrix):
    layers = stiffness.shape[0]
    corner_views = []
    for c in range(8):
        view = lax.slice_in_dim(extended, c // 4, c // 4 + layers, axis=1)
        if c % 2:
            view = shift_ahead(view, 2)
        if c // 2 % 2:
            view = shift_ahead(view, 3)
        corner_views.append(view)
    stacked = jnp.stack(corner_views)
    forces = (
        jnp.einsum("cadb,dbzxy->cazxy", matrix, stacked, precision=lax.Precision.HIGHEST)
        * stiffness
    )
    result = jnp.zeros(extended.shape, jnp.float32)
    for c in range(8):
        piece = forces[c]
        if c % 2:
            piece = shift_behind(piece, 2)
        if c // 2 % 2:
            piece = shift_behind(piece, 3)
        result = result.at[:, c // 4 : c // 4 + layers].add(piece)
    return result


def apply_operator(columns, free_mask, stiffness):
    matrix = jnp.asarray(element_matrix(), dtype=jnp.float32)
    moved = columns * free_mask
    upper = from_behind(moved[:, :, :1], "slab", -1)
    extended = jnp.concatenate([moved, upper], axis=2)

    def per_column(column):
        return element_forces(column, stiffness, matrix)

    forces_out = lax.map(per_column, extended)
    spilled = from_behind(forces_out[:, :, -1:], "slab", 1)
    interior = jnp.concatenate([forces_out[:, :, :1] + spilled, forces_out[:, :, 1:-1]], axis=2)
    return free_mask * interior + (1.0 - free_mask) * columns


def factor_gram(gram_matrix, total_cols):
    cholesky_lower = jnp.linalg.cholesky(gram_matrix)
    inverse = lax.linalg.triangular_solve(
        cholesky_lower, jnp.eye(total_cols, dtype=jnp.float32), left_side=True, lower=True
    )
    return (cholesky_lower, inverse)


def on_device(recycle_basis, densities, solid_mask, fixed_mask):
    layers = recycle_basis.shape[2]
    slab_count = lax.axis_size("slab")
    col_count = lax.axis_size("col")
    own_count = recycle_basis.shape[0]
    total_cols = own_count * col_count
    col_first = lax.axis_index("col") * own_count
    free_mask = 1.0 - fixed_mask.astype(jnp.float32)
    stiffness = element_stiffness(
        densities, solid_mask, lax.axis_index("slab") * layers, layers * slab_count
    )
    gathered = lax.all_gather(recycle_basis, "col", axis=0, tiled=True)
    image_full = apply_operator(gathered, free_mask, stiffness)
    flattened = image_full.reshape(total_cols, -1)
    rows_total = flattened.shape[1] * slab_count
    gram_part = lax.dot_general(
        flattened,
        flattened,
        (((1,), (1,)), ((), ())),
        precision=lax.Precision.HIGHEST,
        preferred_element_type=jnp.float32,
    )
    gram_matrix = lax.psum(gram_part, "slab")
    gram_matrix = gram_matrix / rows_total
    cholesky_lower, inverse = factor_gram(gram_matrix, total_cols)
    own_inverse = lax.dynamic_slice_in_dim(inverse, col_first, own_count, 0)
    ortho = jnp.dot(
        own_inverse, flattened, precision=lax.Precision.HIGHEST, preferred_element_type=jnp.float32
    ).reshape(recycle_basis.shape)
    renewed = jnp.dot(
        own_inverse,
        gathered.reshape(total_cols, -1),
        precision=lax.Precision.HIGHEST,
        preferred_element_type=jnp.float32,
    ).reshape(recycle_basis.shape)
    return (ortho, renewed, cholesky_lower.T)


def solution(mesh):
    placed = (
        P("col", None, "slab", None, None),
        P("slab", None, None),
        P("slab", None, None),
        P("slab", None, None),
    )
    return jax.shard_map(
        on_device,
        mesh=mesh,
        in_specs=placed,
        out_specs=(P("col", None, "slab", None, None), P("col", None, "slab", None, None), P()),
        check_vma=False,
    )
```

profile of v0, /device:TPU:1, one launch (start us, length us, event | category | flops | bytes accessed | tf_op | source)
XLA Modules:
  0.0 229.1 jit_solution(9076592694379909722)
XLA Ops:
  0.6 13.1 %all_gather.3 = f32[16,3,2,8,256]{4,3,2,1,0:T(8,128)S(1)} all-gather(f32[4,3,2,8,256]{4,3,2,1,0:T(8,128)} %param.23), channel_id=1, replica_groups=mesh['slab'=64,'col'=4] {'col'}, dimensions={0}, use_global_device_ids=true | all-gather | bytes 983040 | tf_op jit(solution)/shard_map/all_gather | solution.py:141
  13.7 0.7 broadcast_subtract_fusion
  14.6 6.2 %collective-permute-start = (f32[16,3,1,8,256]{4,3,2,1,0:T(8,128)S(1)}, f32[16,3,1,8,256]{4,3,2,1,0:T(8,128)S(1)}, u32[]{:S(2)}, u32[]{:S(2)}) collective-permute-start(f32[16,3,1,8,256]{4,3,2,1,0:T(8,128)S(1)} %slice.472), channel_id=1, source_target_pairs={{4,0},{8,4},{12,8},{16,12},{20,16},{24,20},{28,24},{32,28},{36,32}... | collective-permute-start | bytes 1179656 | tf_op jit(solution)/shard_map/ppermute | solution.py:13
  20.9 4.5 %collective-permute-done = f32[16,3,1,8,256]{4,3,2,1,0:T(8,128)S(1)} collective-permute-done((f32[16,3,1,8,256]{4,3,2,1,0:T(8,128)S(1)}, f32[16,3,1,8,256]{4,3,2,1,0:T(8,128)S(1)}, u32[]{:S(2)}, u32[]{:S(2)}) %collective-permute-start) | collective-permute-done | bytes 393248 | tf_op jit(solution)/shard_map/ppermute | solution.py:13
  25.5 54.7 %while.21 = (s32[]{:T(128)}, f32[16,3,3,8,256]{4,3,2,1,0:T(8,128)}, f32[16,3,3,8,256]{4,3,2,1,0:T(8,128)S(1)}, f32[2,8,256]{2,1,0:T(8,128)S(1)}, s32[]{:T(128)}, /*index=5*/f32[8,3,8,3,1,1]{2,0,3,1,5,4:T(8,128)S(1)}, f32[]{:T(128)}) while((s32[]{:T(128)}, f32[16,3,3,8,256]{4,3,2,1,0:T(8,128)}, ...), condition=%wide.region_1.2_spmd.clone, body=%wide.region_0.1_spmd.sunk.clone.sunk | while | flops 28569600 | bytes 7303765 | solution.py:116
  26.3 0.6 stack.73
  26.9 0.5 fusion.39
  28.3 0.6 constant_dynamic-update-slice_fusion.5
  29.7 0.6 stack.73
  31.7 0.6 constant_dynamic-update-slice_fusion.5
  33.1 0.6 stack.73
  35.1 0.6 constant_dynamic-update-slice_fusion.5
  36.5 0.6 stack.73
  37.2 0.5 fusion.39
  38.6 0.6 constant_dynamic-update-slice_fusion.5
  40.0 0.6 stack.73
  40.6 0.5 fusion.39
  42.0 0.6 constant_dynamic-update-slice_fusion.5
  43.4 0.6 stack.73
  44.0 0.5 fusion.39
  45.4 0.6 constant_dynamic-update-slice_fusion.5
  46.8 0.6 stack.73
  48.8 0.6 constant_dynamic-update-slice_fusion.5
  50.2 0.6 stack.73
  50.9 0.5 fusion.39
  52.2 0.6 constant_dynamic-update-slice_fusion.5
  53.6 0.6 stack.73
  54.3 0.5 fusion.39
  55.7 0.6 constant_dynamic-update-slice_fusion.5
  57.1 0.6 stack.73
  57.7 0.5 fusion.39
  59.1 0.6 constant_dynamic-update-slice_fusion.5
  60.5 0.6 stack.73
  61.1 0.5 fusion.39
  62.5 0.6 constant_dynamic-update-slice_fusion.5
  63.9 0.6 stack.73
  64.5 0.5 fusion.39
  65.9 0.6 constant_dynamic-update-slice_fusion.5
  67.3 0.6 stack.73
  69.3 0.6 constant_dynamic-update-slice_fusion.5
  70.7 0.6 stack.73
  71.4 0.5 fusion.39
  72.7 0.6 constant_dynamic-update-slice_fusion.5
  74.1 0.6 stack.73
  74.8 0.5 fusion.39
  76.2 0.6 constant_dynamic-update-slice_fusion.5
  77.6 0.6 stack.73
  78.2 0.5 fusion.39
  79.6 0.6 constant_dynamic-update-slice_fusion.5
  80.2 1.0 slice.399
  81.2 1.9 collective-permute-start.1
  83.2 4.7 %collective-permute-done.1 = f32[16,3,1,8,256]{4,3,2,1,0:T(8,128)S(1)} collective-permute-done((f32[16,3,1,8,256]{4,3,2,1,0:T(8,128)S(1)}, f32[16,3,1,8,256]{4,3,2,1,0:T(8,128)S(1)}, u32[]{:S(2)}, u32[]{:S(2)}) %collective-permute-start.1) | collective-permute-done | bytes 393248 | tf_op jit(solution)/shard_map/ppermute | solution.py:13
  87.9 1.2 slice_add_fusion.1
  89.3 1.4 convolution_bitcast_fusion.1
  90.8 130.1 %psum.7 = f32[16,16]{0,1:T(8,128)S(1)} all-reduce(f32[16,16]{0,1:T(8,128)S(1)} %convolution_bitcast_fusion.1), channel_id=1, replica_groups=mesh['slab'=64,'col'=4] {'slab'}, use_global_device_ids=true, to_apply=%region_2.3 | all-reduce | flops 256 | bytes 2048 | tf_op jit(solution)/shard_map/psum | solution.py:152
  220.9 1.5 cholesky.17
  222.4 0.6 compare_reduce_fusion
  223.1 0.6 fusion.16
  223.7 1.2 custom-call.6
  225.2 0.9 fusion.5
  226.1 0.7 copy.316
  226.8 0.9 fusion.7
  227.7 0.7 copy.315
  228.4 0.7 copy.317
  (601 shorter events, 24.8 us)
Async XLA Ops:
  14.5 6.3 %copy-start.1 = (f32[2,8,256]{2,1,0:T(8,128)S(1)}, f32[2,8,256]{2,1,0:T(8,128)}, u32[]{:S(2)}) copy-start(f32[2,8,256]{2,1,0:T(8,128)} %param.24) | copy-start | bytes 49156
  14.5 6.3 %copy-start.2 = (s32[2,8,256]{2,1,0:T(8,128)S(1)}, s32[2,8,256]{2,1,0:T(8,128)}, u32[]{:S(2)}) copy-start(s32[2,8,256]{2,1,0:T(8,128)} %param.25) | copy-start | bytes 49156
  14.6 10.8 %collective-permute-start = (f32[16,3,1,8,256]{4,3,2,1,0:T(8,128)S(1)}, f32[16,3,1,8,256]{4,3,2,1,0:T(8,128)S(1)}, u32[]{:S(2)}, u32[]{:S(2)}) collective-permute-start(f32[16,3,1,8,256]{4,3,2,1,0:T(8,128)S(1)} %slice.472), channel_id=1, source_target_pairs={{4,0},{8,4},{12,8},{16,12},{20,16},{24,20},{28,24},{32,28},{36,32}... | collective-permute-start | bytes 1179656 | tf_op jit(solution)/shard_map/ppermute | solution.py:13
  20.9 4.6 %copy-start = (f32[8,3,8,3,1,1]{2,0,3,1,5,4:T(8,128)S(1)}, f32[8,3,8,3,1,1]{2,0,3,1,5,4:T(8,128)}, u32[]{:S(2)}) copy-start(f32[8,3,8,3,1,1]{2,0,3,1,5,4:T(8,128)} %constant.380) | copy-start | bytes 6916
  81.2 6.6 %collective-permute-start.1 = (f32[16,3,1,8,256]{4,3,2,1,0:T(8,128)S(1)}, f32[16,3,1,8,256]{4,3,2,1,0:T(8,128)S(1)}, u32[]{:S(2)}, u32[]{:S(2)}) collective-permute-start(f32[16,3,1,8,256]{4,3,2,1,0:T(8,128)S(1)} %slice.399), channel_id=1, source_target_pairs={{0,4},{4,8},{8,12},{12,16},{16,20},{20,24},{24,28},{28,32},{32,36}... | collective-permute-start | bytes 1179656 | tf_op jit(solution)/shard_map/ppermute | solution.py:13
where the time goes:
time: 229 us
  blocking collectives  143 us (62%)
  local copies, waits for them, and re-layouts  39.3 us (17%)
  other arithmetic  12.7 us (6%)
  matrix products  11.7 us (5%)
  waiting for transfers between devices  9.18 us (4%)
  starting transfers between devices  8.08 us (4%)
  loops' own time  4.12 us (2%)
    psum x1, blocking collectives, on_device(): gram_matrix = lax.psum(gram_part, 'slab')  130 us
    another operation x224, local copies, waits for them, and re-layouts, element_forces(): stacked = jnp.stack(corner_views)  17.6 us
    all_gather x1, blocking collectives, on_device(): gathered = lax.all_gather(recycle_basis, 'col', axis=0, tiled=True)  13.1 us
    dynamic_update_slice x16, local copies, waits for them, and re-layouts, apply_operator(): forces_out = lax.map(per_column, extended)  10.2 us
    ppermute x2, waiting for transfers between devices, from_behind(): lax.ppermute(value, axis, [(source, source + steps) for source in range(f...  9.18 us
    dot_general x16, matrix products, element_forces(): jnp.einsum('cadb,dbzxy->cazxy', matrix, stacked, precision=lax.Precision....  8.3 us
    ppermute x2, starting transfers between devices, from_behind(): lax.ppermute(value, axis, [(source, source + steps) for source in range(f...  8.08 us
    scatter-add x112, other arithmetic, element_forces(): result = result.at[:, c // 4:c // 4 + layers].add(piece)  6.21 us
  transfers between devices with their start and end apart: 2, of which 2 were waited for; matrix products, arithmetic and copies ran while one was open for 0% of the time, Pallas kernels for 0%

commit v1 on v0

v1 whole, which is shorter than its diff:
```python
import functools

import jax
import jax.numpy as jnp
import numpy as np
from jax import lax
from jax.experimental import pallas as pl
from jax.experimental.pallas import tpu as pltpu
from jax.sharding import PartitionSpec as P

void_stiffness = 0.001
MESH = pl.DeviceIdType.MESH
f32 = jnp.float32


def element_matrix():
    poisson = 0.3
    lame_first = poisson / ((1.0 + poisson) * (1.0 - 2.0 * poisson))
    shear_mod = 1.0 / (2.0 * (1.0 + poisson))
    elastic = np.zeros((6, 6))
    elastic[:3, :3] = lame_first
    for k in range(3):
        elastic[k, k] = lame_first + 2.0 * shear_mod
    for k in range(3, 6):
        elastic[k, k] = shear_mod
    points = [(1.0 - 1.0 / np.sqrt(3.0)) / 2.0, (1.0 + 1.0 / np.sqrt(3.0)) / 2.0]
    matrix = np.zeros((24, 24))
    for a in points:
        for b in points:
            for d in points:
                strain = np.zeros((6, 24))
                for c in range(8):
                    ox, oy, oz = (c % 2, c // 2 % 2, c // 4)
                    weight_x = a if ox else 1.0 - a
                    weight_y = b if oy else 1.0 - b
                    weight_z = d if oz else 1.0 - d
                    slope_x = (1.0 if ox else -1.0) * weight_y * weight_z
                    slope_y = (1.0 if oy else -1.0) * weight_x * weight_z
                    slope_z = (1.0 if oz else -1.0) * weight_x * weight_y
                    strain[0, 3 * c] = slope_x
                    strain[1, 3 * c + 1] = slope_y
                    strain[2, 3 * c + 2] = slope_z
                    strain[3, 3 * c] = slope_y
                    strain[3, 3 * c + 1] = slope_x
                    strain[4, 3 * c + 1] = slope_z
                    strain[4, 3 * c + 2] = slope_y
                    strain[5, 3 * c] = slope_z
                    strain[5, 3 * c + 2] = slope_x
                matrix = matrix + strain.T @ elastic @ strain / 8.0
    return matrix.reshape(8, 3, 8, 3)


def mode_constants():
    signs = np.ones((8, 8))
    for m in range(8):
        for c in range(8):
            for bit in range(3):
                if m >> bit & 1 and not c >> bit & 1:
                    signs[m, c] *= -1.0
    modes = np.einsum("mc,cadb,nd->manb", signs, element_matrix(), signs) / 64.0
    alpha, beta = modes[1, 0, 1, 0], modes[1, 0, 2, 1]
    gamma, delta = modes[3, 1, 3, 1], modes[3, 1, 5, 2]
    shear, twist = modes[2, 0, 2, 0], modes[7, 2, 7, 2]
    eta_diag, eta = modes[6, 0, 6, 0], modes[6, 0, 5, 1]
    return [float(v) for v in (alpha - beta, beta, gamma, delta, shear, twist, eta_diag - eta, eta)]


def next_along_y(first, second, lane):
    a, b = (pltpu.roll(first, 127, axis=1), pltpu.roll(second, 127, axis=1))
    return (jnp.where(lane == 127, b, a), jnp.where(lane == 127, a, b))


def prior_along_y(first, second, lane):
    a, b = (pltpu.roll(first, 1, axis=1), pltpu.roll(second, 1, axis=1))
    return (jnp.where(lane == 0, b, a), jnp.where(lane == 0, a, b))


def column_image(layers, scaled, lane):
    fields = {}
    for l in range(4):
        for a in range(3):
            v = layers[l][a]
            halves = (v[:, :128], v[:, 128:])
            ahead = next_along_y(halves[0], halves[1], lane)
            for h in range(2):
                fields[l, a, h] = (halves[h] + ahead[h], ahead[h] - halves[h])

    def planes(l, a, h):
        out = []
        for f in fields[l, a, h]:
            g = pltpu.roll(f, 7, axis=0)
            out.append((f + g, g - f))
        return {0: out[0][0], 1: out[0][1], 2: out[1][0], 3: out[1][1]}

    partial = {}
    for h in range(2):
        below = [planes(0, a, h) for a in range(3)]
        acc = {}

        def add(key, value):
            acc[key] = acc[key] + value if key in acc else value

        for e in range(3):
            above = [planes(e + 1, a, h) for a in range(3)]

            def mode(a, m):
                lo, hi = (below[a][m & 3], above[a][m & 3])
                return hi - lo if m & 4 else hi + lo

            def stiff(k):
                return scaled[e, k, :, 128 * h : 128 * h + 128]

            force = {}
            x, y, z = (mode(0, 1), mode(1, 2), mode(2, 4))
            shared = (x + y + z) * stiff(1)
            force[0, 1] = x * stiff(0) + shared
            force[1, 2] = y * stiff(0) + shared
            force[2, 4] = z * stiff(0) + shared
            for a, b, p in ((1, 2, 1), (0, 2, 2), (0, 1, 4)):
                ma, mb = (p ^ (1 << a), p ^ (1 << b))
                q, r = (mode(a, ma), mode(b, mb))
                force[a, ma] = q * stiff(2) + r * stiff(3)
                force[b, mb] = r * stiff(2) + q * stiff(3)
            for a, b, c in ((0, 1, 2), (0, 2, 1), (1, 2, 0)):
                ma, mb = (1 << b, 1 << a)
                force[a, ma] = force[b, mb] = None
                both = (mode(a, ma) + mode(b, mb)) * stiff(4)
                force[a, ma] = force[b, mb] = both
                force[c, 7] = mode(c, 7) * stiff(5)
            x, y, z = (mode(0, 6), mode(1, 5), mode(2, 3))
            shared = (x + y + z) * stiff(7)
            force[0, 6] = x * stiff(6) + shared
            force[1, 5] = y * stiff(6) + shared
            force[2, 3] = z * stiff(6) + shared
            for a in range(3):
                for m in range(4):
                    high = force[a, m + 4]
                    low = force.get((a, m))
                    if e >= 1:
                        add((e - 1, a, m), -high if low is None else low - high)
                    if e <= 1:
                        add((e, a, m), high if low is None else low + high)
            below = above
        for l in range(2):
            for a in range(3):
                g = [acc[l, a, m] for m in range(4)]
                total = (g[0] - g[1]) + pltpu.roll(g[0] + g[1], 1, axis=0)
                slope = (g[2] - g[3]) + pltpu.roll(g[2] + g[3], 1, axis=0)
                partial[l, a, h] = (total - slope, total + slope)
    result = {}
    for l in range(2):
        for a in range(3):
            moved = prior_along_y(partial[l, a, 0][1], partial[l, a, 1][1], lane)
            result[l, a] = jnp.concatenate(
                [partial[l, a, 0][0] + moved[0], partial[l, a, 1][0] + moved[1]], axis=1
            )
    return result


def split_bf16(value, parts):
    out = []
    for _ in range(parts):
        piece = value.astype(jnp.bfloat16)
        out.append(piece)
        value = value - piece.astype(f32)
    return out


def body(
    slabs, cols, constants, rows_total,
    u_hbm, dens_hbm, solid_hbm, fixed_hbm,
    ortho_ref, renew_ref, r_ref,
    u_all, im_all, halo, dens, solid, fixed, scaled, gram_a, gram_b, rows_ref, coef_ref,
    local_sem, halo_send, halo_recv, ag_send, ag_recv, im_send, im_recv, ga_send, ga_recv, gb_send, gb_recv,
):
    s = lax.axis_index("slab")
    c = lax.axis_index("col")
    group = 8
    zi, yc = s // group, s % group
    zn = slabs // group

    def slab_at(value):
        return {"slab": value, "col": c}

    up, down = (lax.rem(s + 1, slabs), lax.rem(s + slabs - 1, slabs))
    partners = [slab_at(up), slab_at(down)]
    partners += [{"slab": s, "col": lax.rem(c + k, cols)} for k in range(1, cols)]
    partners += [slab_at(zi * group + lax.rem(yc + k, group)) for k in range(1, group)]
    partners += [slab_at(lax.rem(zi + k, zn) * group + yc) for k in range(1, zn)]

    local = [
        pltpu.make_async_copy(u_hbm, u_all.at[c], local_sem.at[0]),
        pltpu.make_async_copy(dens_hbm, dens.at[pl.ds(1, 2)], local_sem.at[1]),
        pltpu.make_async_copy(solid_hbm, solid.at[pl.ds(1, 2)], local_sem.at[2]),
        pltpu.make_async_copy(fixed_hbm, fixed.at[pl.ds(1, 2)], local_sem.at[3]),
    ]
    for copy in local:
        copy.start()

    barrier = pltpu.get_barrier_semaphore()
    for partner in partners:
        pl.semaphore_signal(barrier, inc=1, device_id=partner, device_id_type=MESH)
    pl.semaphore_wait(barrier, len(partners))

    def remote(src, dst, send, recv, where):
        return pltpu.make_async_remote_copy(
            src_ref=src, dst_ref=dst, send_sem=send, recv_sem=recv, device_id=where, device_id_type=MESH
        )

    halo_copies = []
    for k, (src, dst, where) in enumerate((
        (u_hbm.at[:, :, 1], halo.at[0], slab_at(up)),
        (u_hbm.at[:, :, 0], halo.at[1], slab_at(down)),
        (dens_hbm.at[1], dens.at[0], slab_at(up)),
        (solid_hbm.at[1], solid.at[0], slab_at(up)),
        (fixed_hbm.at[1], fixed.at[0], slab_at(up)),
        (fixed_hbm.at[0], fixed.at[3], slab_at(down)),
    )):
        halo_copies.append(remote(src, dst, halo_send.at[k], halo_recv.at[k], where))
    for copy in halo_copies:
        copy.start()

    ag_copies = [
        remote(u_hbm, u_all.at[c], ag_send.at[k], ag_recv.at[k], {"slab": s, "col": lax.rem(c + k, cols)})
        for k in range(1, cols)
    ]
    ag_copies[0].start()
    ag_copies[cols - 2].start()

    for copy in local:
        copy.wait()
    for copy in halo_copies:
        copy.wait()

    node = lax.broadcasted_iota(jnp.int32, (8, 256), 0)
    along = lax.broadcasted_iota(jnp.int32, (8, 256), 1)
    inside = (node < 7) & (along < 255)
    for e in range(3):
        depth = s * 2 - 1 + e
        value = solid[e].astype(f32) * (dens[e] * dens[e] * dens[e]) + void_stiffness
        keep = inside & (depth >= 0) & (depth < 2 * slabs - 1)
        value = jnp.where(keep, value, 0.0)
        for k, constant in enumerate(constants):
            scaled[e, k] = value * constant

    lane = lax.broadcasted_iota(jnp.int32, (8, 128), 1)

    def one_column(j, carry):
        free = [1.0 - fixed[l].astype(f32) for l in range(4)]
        raw = [[u_all[c, j, a, l] for a in range(3)] for l in range(2)]
        layers = [
            [halo[0, j, a] * free[0] for a in range(3)],
            [raw[0][a] * free[1] for a in range(3)],
            [raw[1][a] * free[2] for a in range(3)],
            [halo[1, j, a] * free[3] for a in range(3)],
        ]
        out = column_image(layers, scaled, lane)
        for l in range(2):
            for a in range(3):
                im_all[c, j, a, l] = free[l + 1] * out[l, a] + (1.0 - free[l + 1]) * raw[l][a]
        return carry

    lax.fori_loop(0, 4, one_column, 0)

    im_copies = [
        remote(im_all.at[c], im_all.at[c], im_send.at[k], im_recv.at[k], {"slab": s, "col": lax.rem(c + k, cols)})
        for k in range(1, cols)
    ]
    for copy in im_copies:
        copy.start()
    for copy in im_copies:
        copy.wait()
    for copy in ag_copies[1 : cols - 2]:
        copy.start()

    total = None
    for a in range(3):
        for l in range(2):
            block = im_all[:, :, a, l].reshape(128, 256)
            both = jnp.concatenate(split_bf16(block, 2), axis=0)
            part = lax.dot_general(both, both, (((1,), (1,)), ((), ())), preferred_element_type=f32)
            total = part if total is None else total + part
    pairs = (total[:128, :128] + total[128:, 128:]) + (total[:128, 128:] + total[128:, :128])
    row_id = lax.broadcasted_iota(jnp.int32, (128, 128), 0)
    col_id = lax.broadcasted_iota(jnp.int32, (128, 128), 1)
    pairs = jnp.where(row_id % 8 == col_id % 8, pairs, 0.0)
    partial = pairs.reshape(16, 8, 128).sum(axis=1)

    gram_a[yc] = partial
    ga_copies = [
        remote(gram_a.at[yc], gram_a.at[yc], ga_send.at[k], ga_recv.at[k], slab_at(zi * group + lax.rem(yc + k, group)))
        for k in range(1, group)
    ]
    for copy in ga_copies:
        copy.start()
    for copy in ga_copies:
        copy.wait()
    summed = gram_a[0]
    for k in range(1, group):
        summed = summed + gram_a[k]
    gram_b[zi] = summed
    gb_copies = [
        remote(gram_b.at[zi], gram_b.at[zi], gb_send.at[k], gb_recv.at[k], slab_at(lax.rem(zi + k, zn) * group + yc))
        for k in range(1, zn)
    ]
    for copy in gb_copies:
        copy.start()
    for copy in gb_copies:
        copy.wait()
    summed = gram_b[0]
    for k in range(1, zn):
        summed = summed + gram_b[k]

    picked = (row_id // 8 == col_id).astype(jnp.bfloat16)
    gram = None
    for piece in split_bf16(summed, 3)[::-1]:
        part = jnp.dot(piece, picked, preferred_element_type=f32)
        gram = part if gram is None else gram + part
    gram = gram * (1.0 / rows_total)

    row16 = lax.broadcasted_iota(jnp.int32, (16, 128), 0)
    lane16 = lax.broadcasted_iota(jnp.int32, (16, 128), 1)
    work = jnp.where(lane16 < 16, gram, (lane16 == row16 + 16).astype(f32))
    for k in range(16):
        pivot = work[k : k + 1, k : k + 1]
        scale = lax.rsqrt(pivot)
        scale = scale * (1.5 - 0.5 * pivot * scale * scale)
        row = work[k : k + 1, :] * scale
        rows_ref[k : k + 1, :] = row
        if k < 15:
            work = work - (work[:, k : k + 1] * scale) * row
    factor = rows_ref[...]
    r_ref[...] = jnp.where(lane16 >= row16, factor, 0.0)[:, :16]

    own = rows_ref[pl.ds(4 * c, 4), :]
    for i in range(4):
        for j in range(16):
            coef_ref[i, j] = jnp.broadcast_to(own[i : i + 1, 16 + j : 17 + j], (8, 256))

    for copy in ag_copies:
        copy.wait()

    def combine(step, carry):
        a, l = step // 2, step % 2
        for source, target in ((u_all, renew_ref), (im_all, ortho_ref)):
            acc = [None] * 4
            for j in range(16):
                value = source[j // 4, j % 4, a, l]
                for i in range(4):
                    term = coef_ref[i, j] * value
                    acc[i] = term if acc[i] is None else acc[i] + term
            for i in range(4):
                target[i, a, l] = acc[i]
        return carry

    lax.fori_loop(0, 6, combine, 0)


def solution(mesh):
    slabs, cols = (mesh.shape["slab"], mesh.shape["col"])
    constants = mode_constants()

    def on_device(recycle_basis, densities, solid_mask, fixed_mask):
        shape = recycle_basis.shape
        rows_total = 3 * slabs * shape[2] * shape[3] * shape[4]
        vmem = pl.BlockSpec(memory_space=pltpu.VMEM)
        hbm = pl.BlockSpec(memory_space=pl.ANY)
        dma = pltpu.SemaphoreType.DMA
        layer = shape[3:]
        return pl.pallas_call(
            functools.partial(body, slabs, cols, constants, float(rows_total)),
            out_shape=(
                jax.ShapeDtypeStruct(shape, f32),
                jax.ShapeDtypeStruct(shape, f32),
                jax.ShapeDtypeStruct((16, 16), f32),
            ),
            in_specs=[hbm] * 4,
            out_specs=(vmem, vmem, vmem),
            scratch_shapes=[
                pltpu.VMEM((cols,) + shape, f32),
                pltpu.VMEM((cols,) + shape, f32),
                pltpu.VMEM((2, 4, 3) + layer, f32),
                pltpu.VMEM((3,) + layer, f32),
                pltpu.VMEM((3,) + layer, jnp.int32),
                pltpu.VMEM((4,) + layer, jnp.int32),
                pltpu.VMEM((3, len(constants)) + layer, f32),
                pltpu.VMEM((8, 16, 128), f32),
                pltpu.VMEM((8, 16, 128), f32),
                pltpu.VMEM((16, 128), f32),
                pltpu.VMEM((4, 16, 8, 256), f32),
                dma((4,)), dma((6,)), dma((6,)),
                dma((4,)), dma((4,)), dma((4,)), dma((4,)),
                dma((8,)), dma((8,)), dma((8,)), dma((8,)),
            ],
            compiler_params=pltpu.CompilerParams(collective_id=0, has_side_effects=True),
        )(recycle_basis, densities, solid_mask, fixed_mask)

    placed = (
        P("col", None, "slab", None, None),
        P("slab", None, None),
        P("slab", None, None),
        P("slab", None, None),
    )
    return jax.shard_map(
        on_device,
        mesh=mesh,
        in_specs=placed,
        out_specs=(P("col", None, "slab", None, None), P("col", None, "slab", None, None), P()),
        check_vma=False,
    )
```

time: 229 us -> 41.4 us (0.18)
  blocking collectives: 143 us -> 0 us
  Pallas kernels: 0 us -> 37.7 us
  local copies, waits for them, and re-layouts: 39.3 us -> 2.95 us
  other arithmetic: 12.7 us -> 0 us
  matrix products: 11.7 us -> 0 us
  waiting for transfers between devices: 9.18 us -> 0 us
  starting transfers between devices: 8.08 us -> 0 us
  loops' own time: 4.12 us -> 0 us
    psum x1 -> x0, blocking collectives: 130 us -> none  [on_device(): gram_matrix = lax.psum(gram_part, 'slab')]
    pallas_call x0 -> x1, Pallas kernels: none -> 37.7 us  [on_device(): pl.pallas_call(functools.partial(body, slabs, cols, constants, float(rows...]
    another operation x224 -> x0, local copies, waits for them, and re-layouts: 17.6 us -> none  [element_forces(): stacked = jnp.stack(corner_views)]
    all_gather x1 -> x0, blocking collectives: 13.1 us -> none  [on_device(): gathered = lax.all_gather(recycle_basis, 'col', axis=0, tiled=True)]
    dot_general x19 -> x0, matrix products: 11.6 us -> none  [the longest x16 8.3 us: element_forces(): jnp.einsum('cadb,dbzxy->cazxy', matrix, stacked, precision=lax.Precision....]
    dynamic_update_slice x16 -> x0, local copies, waits for them, and re-layouts: 10.2 us -> none  [apply_operator(): forces_out = lax.map(per_column, extended)]
    ppermute x2 -> x0, waiting for transfers between devices: 9.18 us -> none  [from_behind(): lax.ppermute(value, axis, [(source, source + steps) for source in range(f...]
    slice x210 -> x0, local copies, waits for them, and re-layouts: 9.04 us -> none  [the longest x128 4.83 us: element_forces(): piece = forces[c]]
  transfers between devices with their start and end apart: 2 -> 0, of which waited for: 2 -> 0; matrix products, arithmetic and copies ran while one was open for 0% -> 0% of each run, Pallas kernels for 0% -> 0%
where the time goes in v1:
time: 41.4 us; the launch traced here: 41.3 us
  Pallas kernels  37.7 us (91%)
  local copies, waits for them, and re-layouts  2.95 us (7%)
  between operations  0.65 us (2%)
    pallas_call x1, Pallas kernels, on_device(): pl.pallas_call(functools.partial(body, slabs, cols, constants, float(rows...  37.7 us
    unnamed x7, local copies, waits for them, and re-layouts  2.95 us

profile of v1, /device:TPU:1, one launch (start us, length us, event | category | flops | bytes accessed | tf_op | source)
XLA Modules:
  0.0 41.3 jit_solution(14292405048983135616)
XLA Ops:
  0.6 37.7 %shard_map.67 = (f32[4,3,2,8,256]{4,3,2,1,0:T(8,128)}, f32[4,3,2,8,256]{4,3,2,1,0:T(8,128)}, f32[16,16]{1,0:T(8,128)}) custom-call(f32[4,3,2,8,256]{4,3,2,1,0:T(8,128)} %u_hbm.1, f32[2,8,256]{2,1,0:T(8,128)} %dens_hbm.1, s32[2,8,256]{2,1,0:T(8,128)} %solid_hbm.1, s32[2,8,256]{2,1,0:T(8,128)} %fixed_hbm.1), custom_call_target="tpu_custom_call" | custom-call | tf_op jit(solution)/shard_map/pallas_call | solution.py:370
  38.3 0.0 copy-start
  38.3 1.7 %copy.10 = f32[4,3,2,8,256]{4,3,2,1,0:T(8,128)} copy(f32[4,3,2,8,256]{4,3,2,1,0:T(8,128)} %get-tuple-element.6) | data formatting | bytes 393216
  40.0 0.0 copy-done
  40.0 0.0 copy-start.1
  40.0 0.7 %copy.11 = f32[4,3,2,8,256]{4,3,2,1,0:T(8,128)} copy(f32[4,3,2,8,256]{4,3,2,1,0:T(8,128)S(1)} %copy-done) | data formatting | bytes 393216
  40.6 0.0 copy-done.1
  40.7 0.6 %copy.12 = f32[16,16]{1,0:T(8,128)} copy(f32[16,16]{1,0:T(8,128)S(1)} %copy-done.1) | data formatting | bytes 2048
Async XLA Ops:
  38.3 1.7 %copy-start = (f32[4,3,2,8,256]{4,3,2,1,0:T(8,128)S(1)}, f32[4,3,2,8,256]{4,3,2,1,0:T(8,128)}, u32[]{:S(2)}) copy-start(f32[4,3,2,8,256]{4,3,2,1,0:T(8,128)} %get-tuple-element.7) | copy-start | bytes 589828
  40.0 0.7 %copy-start.1 = (f32[16,16]{1,0:T(8,128)S(1)}, f32[16,16]{1,0:T(8,128)}, u32[]{:S(2)}) copy-start(f32[16,16]{1,0:T(8,128)} %get-tuple-element.8) | copy-start | bytes 3076

commit v2 on v1

--- a/solution.py
+++ b/solution.py
@@ -166,27 +166,40 @@
     return out
 
 
-def body(
+def exact_dot(value, ones):
+    rows = value.shape[0]
+    parts = jnp.dot(jnp.concatenate(split_bf16(value, 3), axis=0), ones, preferred_element_type=f32)
+    return (parts[2 * rows :] + parts[rows : 2 * rows]) + parts[:rows]
+
+
+def exchange(
     slabs, cols, constants, rows_total,
     u_hbm, dens_hbm, solid_hbm, fixed_hbm,
-    ortho_ref, renew_ref, r_ref,
-    u_all, im_all, halo, dens, solid, fixed, scaled, gram_a, gram_b, rows_ref, coef_ref,
-    local_sem, halo_send, halo_recv, ag_send, ag_recv, im_send, im_recv, ga_send, ga_recv, gb_send, gb_recv,
+    u_all, im_all, rows_ref,
+    halo, dens, solid, fixed, scaled, gram_a, gram_b,
+    local_sem, halo_send, halo_recv, u_send, u_recv, q_send, q_recv, im_send, im_recv, gram_send, gram_recv,
+    ready_x, ready_z,
 ):
     s = lax.axis_index("slab")
     c = lax.axis_index("col")
     group = 8
     zi, yc = s // group, s % group
     zn = slabs // group
-
-    def slab_at(value):
-        return {"slab": value, "col": c}
-
-    up, down = (lax.rem(s + 1, slabs), lax.rem(s + slabs - 1, slabs))
-    partners = [slab_at(up), slab_at(down)]
-    partners += [{"slab": s, "col": lax.rem(c + k, cols)} for k in range(1, cols)]
-    partners += [slab_at(zi * group + lax.rem(yc + k, group)) for k in range(1, group)]
-    partners += [slab_at(lax.rem(zi + k, zn) * group + yc) for k in range(1, zn)]
+    wide = cols * group
+
+    def at(slab, col):
+        return {"slab": slab, "col": col}
+
+    def along_x(k):
+        return at(s, lax.rem(c + k + cols, cols))
+
+    def along_z(k):
+        return at(lax.rem(zi + k + zn, zn) * group + yc, c)
+
+    up, down = (at(lax.rem(s + 1, slabs), c), at(lax.rem(s + slabs - 1, slabs), c))
+    near = [up, down, along_z(1), along_z(-1)]
+    near += [along_x(k) for k in range(1, cols)]
+    near += [at(zi * group + lax.rem(yc + k, group), c) for k in range(1, group)]
 
     local = [
         pltpu.make_async_copy(u_hbm, u_all.at[c], local_sem.at[0]),
@@ -194,43 +207,49 @@
         pltpu.make_async_copy(solid_hbm, solid.at[pl.ds(1, 2)], local_sem.at[2]),
         pltpu.make_async_copy(fixed_hbm, fixed.at[pl.ds(1, 2)], local_sem.at[3]),
     ]
+    barrier = pltpu.get_barrier_semaphore()
+    for partner in near:
+        pl.semaphore_signal(barrier, inc=1, device_id=partner, device_id_type=MESH)
     for copy in local:
         copy.start()
-
-    barrier = pltpu.get_barrier_semaphore()
-    for partner in partners:
-        pl.semaphore_signal(barrier, inc=1, device_id=partner, device_id_type=MESH)
-    pl.semaphore_wait(barrier, len(partners))
+    pl.semaphore_wait(barrier, len(near))
 
     def remote(src, dst, send, recv, where):
         return pltpu.make_async_remote_copy(
             src_ref=src, dst_ref=dst, send_sem=send, recv_sem=recv, device_id=where, device_id_type=MESH
         )
 
-    halo_copies = []
-    for k, (src, dst, where) in enumerate((
-        (u_hbm.at[:, :, 1], halo.at[0], slab_at(up)),
-        (u_hbm.at[:, :, 0], halo.at[1], slab_at(down)),
-        (dens_hbm.at[1], dens.at[0], slab_at(up)),
-        (solid_hbm.at[1], solid.at[0], slab_at(up)),
-        (fixed_hbm.at[1], fixed.at[0], slab_at(up)),
-        (fixed_hbm.at[0], fixed.at[3], slab_at(down)),
-    )):
-        halo_copies.append(remote(src, dst, halo_send.at[k], halo_recv.at[k], where))
-    for copy in halo_copies:
-        copy.start()
-
-    ag_copies = [
-        remote(u_hbm, u_all.at[c], ag_send.at[k], ag_recv.at[k], {"slab": s, "col": lax.rem(c + k, cols)})
-        for k in range(1, cols)
-    ]
-    ag_copies[0].start()
-    ag_copies[cols - 2].start()
+    def received(ref, sem):
+        remote(ref, ref, sem, sem, along_x(1)).wait_recv()
+
+    def sent(ref, sem):
+        remote(ref, ref, sem, sem, along_x(1)).wait_send()
+
+    small_send, small_recv = (halo_send.at[4], halo_recv.at[4])
+    remote(dens_hbm.at[1], dens.at[0], small_send, small_recv, up).start()
+    remote(solid_hbm.at[1], solid.at[0], small_send, small_recv, up).start()
+    remote(fixed_hbm.at[1], fixed.at[0], small_send, small_recv, up).start()
+    remote(fixed_hbm.at[0], fixed.at[3], small_send, small_recv, down).start()
+    for j in range(4):
+        remote(u_hbm.at[j, :, 1], halo.at[0, j], halo_send.at[j], halo_recv.at[j], up).start()
+        remote(u_hbm.at[j, :, 0], halo.at[1, j], halo_send.at[j], halo_recv.at[j], down).start()
+
+    first_pair, last_pair = (pl.ds(0, 2), pl.ds(2, 2))
+    u_next = remote(u_hbm, u_all.at[c], u_send.at[0], u_recv.at[0], along_x(1))
+    u_wrap = remote(u_hbm, u_all.at[c], u_send.at[1], u_recv.at[1], along_x(-1))
+    u_back = remote(u_hbm.at[last_pair], u_all.at[c, last_pair], u_send.at[2], u_recv.at[2], along_x(-1))
+    pl.when(c < cols - 1)(u_next.start)
+    pl.when(c == 0)(u_wrap.start)
+    pl.when(c == 1)(u_back.start)
+
+    for k in range(1, cols):
+        pl.semaphore_signal(ready_x, inc=1, device_id=along_x(k), device_id_type=MESH)
+    for k in (1, -1):
+        pl.semaphore_signal(ready_z.at[0], inc=1, device_id=along_z(k), device_id_type=MESH)
 
     for copy in local:
         copy.wait()
-    for copy in halo_copies:
-        copy.wait()
+    received(fixed, small_recv)
 
     node = lax.broadcasted_iota(jnp.int32, (8, 256), 0)
     along = lax.broadcasted_iota(jnp.int32, (8, 256), 1)
@@ -248,6 +267,7 @@
     def one_column(j, carry):
         free = [1.0 - fixed[l].astype(f32) for l in range(4)]
         raw = [[u_all[c, j, a, l] for a in range(3)] for l in range(2)]
+        received(halo.at[:, 0], halo_recv.at[j])
         layers = [
             [halo[0, j, a] * free[0] for a in range(3)],
             [raw[0][a] * free[1] for a in range(3)],
@@ -257,69 +277,95 @@
         out = column_image(layers, scaled, lane)
         for l in range(2):
             for a in range(3):
-                im_all[c, j, a, l] = free[l + 1] * out[l, a] + (1.0 - free[l + 1]) * raw[l][a]
+                value = free[l + 1] * out[l, a] + (1.0 - free[l + 1]) * raw[l][a]
+                im_all[c, j, a, l, 0] = value[:, :128]
+                im_all[c, j, a, l, 1] = value[:, 128:]
+        for k in range(1, cols):
+            t = lax.rem(c + k, cols)
+            piece = im_all.at[c, j, :, t // 2, t % 2]
+            remote(piece, piece, q_send, q_recv, at(s, t)).start()
         return carry
 
     lax.fori_loop(0, 4, one_column, 0)
 
-    im_copies = [
-        remote(im_all.at[c], im_all.at[c], im_send.at[k], im_recv.at[k], {"slab": s, "col": lax.rem(c + k, cols)})
-        for k in range(1, cols)
-    ]
-    for copy in im_copies:
-        copy.start()
-    for copy in im_copies:
-        copy.wait()
-    for copy in ag_copies[1 : cols - 2]:
-        copy.start()
-
+    pl.semaphore_wait(ready_z.at[0], 2)
+    for k in (2, -2):
+        pl.semaphore_signal(ready_z.at[1], inc=1, device_id=along_z(k), device_id_type=MESH)
+    pl.semaphore_wait(ready_x, cols - 1)
+
+    quarters = im_all.at[pl.ds(0, cols - 1), :, :, 0, 0]
+    received(quarters, q_recv)
+
+    mine_l, mine_h = (c // 2, c % 2)
+    sides = []
+    for a in range(3):
+        block = im_all[:, :, a, mine_l, mine_h].reshape(128, 128)
+        sides.append(jnp.concatenate(split_bf16(block, 2), axis=0))
     total = None
-    for a in range(3):
-        for l in range(2):
-            block = im_all[:, :, a, l].reshape(128, 256)
-            both = jnp.concatenate(split_bf16(block, 2), axis=0)
-            part = lax.dot_general(both, both, (((1,), (1,)), ((), ())), preferred_element_type=f32)
-            total = part if total is None else total + part
+    for both in (jnp.concatenate(sides[:2], axis=1), sides[2]):
+        part = lax.dot_general(both, both, (((1,), (1,)), ((), ())), preferred_element_type=f32)
+        total = part if total is None else total + part
     pairs = (total[:128, :128] + total[128:, 128:]) + (total[:128, 128:] + total[128:, :128])
     row_id = lax.broadcasted_iota(jnp.int32, (128, 128), 0)
     col_id = lax.broadcasted_iota(jnp.int32, (128, 128), 1)
-    pairs = jnp.where(row_id % 8 == col_id % 8, pairs, 0.0)
-    partial = pairs.reshape(16, 8, 128).sum(axis=1)
-
-    gram_a[yc] = partial
-    ga_copies = [
-        remote(gram_a.at[yc], gram_a.at[yc], ga_send.at[k], ga_recv.at[k], slab_at(zi * group + lax.rem(yc + k, group)))
-        for k in range(1, group)
-    ]
-    for copy in ga_copies:
-        copy.start()
-    for copy in ga_copies:
-        copy.wait()
-    summed = gram_a[0]
-    for k in range(1, group):
-        summed = summed + gram_a[k]
-    gram_b[zi] = summed
-    gb_copies = [
-        remote(gram_b.at[zi], gram_b.at[zi], gb_send.at[k], gb_recv.at[k], slab_at(lax.rem(zi + k, zn) * group + yc))
-        for k in range(1, zn)
-    ]
-    for copy in gb_copies:
-        copy.start()
-    for copy in gb_copies:
-        copy.wait()
-    summed = gram_b[0]
-    for k in range(1, zn):
-        summed = summed + gram_b[k]
-
-    picked = (row_id // 8 == col_id).astype(jnp.bfloat16)
-    gram = None
-    for piece in split_bf16(summed, 3)[::-1]:
-        part = jnp.dot(piece, picked, preferred_element_type=f32)
-        gram = part if gram is None else gram + part
-    gram = gram * (1.0 / rows_total)
-
+    pairs = jnp.where(row_id % 8 == col_id % 8, pairs, 0.0).reshape(16, 8, 128).sum(axis=1)
     row16 = lax.broadcasted_iota(jnp.int32, (16, 128), 0)
     lane16 = lax.broadcasted_iota(jnp.int32, (16, 128), 1)
+    spread = (row_id // 8 == col_id // 8).astype(jnp.bfloat16)
+    pairs = exact_dot(pairs, spread)
+    packed = jnp.where(row16 % 8 == lane16 % 8, pairs, 0.0).reshape(2, 8, 128).sum(axis=1)
+
+    slot = c * group + yc
+    gram_a[slot] = packed
+    for k in range(1, wide):
+        other = lax.rem(slot + k, wide)
+        remote(
+            gram_a.at[slot], gram_a.at[slot], gram_send.at[0], gram_recv.at[0], at(zi * group + other % group, other // group)
+        ).start()
+
+    for k in range(1, cols):
+        t = lax.rem(c + 1 + k, cols)
+        piece = im_all.at[c, :, :, t // 2, t % 2]
+        pl.when(c < cols - 1)(remote(piece, piece, im_send.at[0], im_recv.at[0], along_x(1)).start)
+        piece = im_all.at[c, :, :, (k - 1) // 2, (k - 1) % 2]
+        pl.when(c == 0)(remote(piece, piece, im_send.at[1], im_recv.at[1], along_x(-1)).start)
+    piece = im_all.at[c, :, :, 1, 0]
+    im_back = remote(piece, piece, im_send.at[2], im_recv.at[2], along_x(-1))
+    pl.when(c == 1)(im_back.start)
+
+    ahead = (c == 1) | (c == 2)
+    relay_block = jnp.where(ahead, c - 1, lax.rem(c + 1, cols))
+    pl.when(c >= 1)(lambda: received(u_all.at[0], u_recv.at[0]))
+    pl.when(c == 3)(lambda: received(u_all.at[0], u_recv.at[1]))
+    pl.when(c == 0)(lambda: received(u_all.at[0, last_pair], u_recv.at[2]))
+    ref = u_all.at[relay_block, first_pair]
+    pl.when(ahead)(remote(ref, ref, u_send.at[3], u_recv.at[3], along_x(1)).start)
+    ref = u_all.at[relay_block, last_pair]
+    pl.when(jnp.logical_not(ahead))(remote(ref, ref, u_send.at[4], u_recv.at[4], along_x(-1)).start)
+
+    received(gram_a.at[pl.ds(0, wide - 1)], gram_recv.at[0])
+    summed = jnp.sum(gram_a[...], axis=0)
+    gram_b[zi] = summed
+    pl.semaphore_wait(ready_z.at[1], 2)
+    for k in range(1, zn):
+        remote(gram_b.at[zi], gram_b.at[zi], gram_send.at[1], gram_recv.at[1], along_z(k)).start()
+
+    pl.when(c >= 1)(lambda: received(quarters, im_recv.at[0]))
+    pl.when(c == 3)(lambda: received(quarters, im_recv.at[1]))
+    pl.when(c == 0)(lambda: received(im_all.at[0, :, :, 0, 0], im_recv.at[2]))
+    ref = im_all.at[relay_block, :, :, 0]
+    pl.when(ahead)(remote(ref, ref, im_send.at[3], im_recv.at[3], along_x(1)).start)
+    ref = im_all.at[relay_block, :, :, 1, jnp.where(c == 3, 1, 0)]
+    pl.when(jnp.logical_not(ahead))(remote(ref, ref, im_send.at[4], im_recv.at[4], along_x(-1)).start)
+
+    received(gram_b.at[pl.ds(0, zn - 1)], gram_recv.at[1])
+    summed = jnp.sum(gram_b[...], axis=0)
+
+    wide_rows = jnp.concatenate([jnp.broadcast_to(summed[r : r + 1], (8, 128)) for r in range(2)], axis=0)
+    kept = jnp.where(row16 % 8 == lane16 % 8, wide_rows, 0.0)
+    picked = (row_id // 8 == col_id).astype(jnp.bfloat16)
+    gram = exact_dot(kept, picked) * (1.0 / rows_total)
+
     work = jnp.where(lane16 < 16, gram, (lane16 == row16 + 16).astype(f32))
     for k in range(16):
         pivot = work[k : k + 1, k : k + 1]
@@ -329,31 +375,72 @@
         rows_ref[k : k + 1, :] = row
         if k < 15:
             work = work - (work[:, k : k + 1] * scale) * row
-    factor = rows_ref[...]
-    r_ref[...] = jnp.where(lane16 >= row16, factor, 0.0)[:, :16]
-
+
+    pl.when((c == 2) | (c == 3))(lambda: received(u_all.at[0, first_pair], u_recv.at[3]))
+    pl.when((c == 2) | (c == 3))(lambda: received(u_all.at[0, first_pair], u_recv.at[4]))
+    pl.when((c == 2) | (c == 3))(lambda: received(im_all.at[0, :, :, 0], im_recv.at[3]))
+    pl.when((c == 2) | (c == 3))(lambda: received(im_all.at[0, :, :, 0, 0], im_recv.at[4]))
+    sent(fixed, small_send)
+    for j in range(4):
+        sent(halo.at[:, 0], halo_send.at[j])
+    sent(quarters, q_send)
+    sent(gram_a.at[pl.ds(0, wide - 1)], gram_send.at[0])
+    sent(gram_b.at[pl.ds(0, zn - 1)], gram_send.at[1])
+    pl.when(c < cols - 1)(lambda: sent(u_all.at[0], u_send.at[0]))
+    pl.when(c == 0)(lambda: sent(u_all.at[0], u_send.at[1]))
+    pl.when(c == 1)(lambda: sent(u_all.at[0, first_pair], u_send.at[2]))
+    pl.when(c < cols - 1)(lambda: sent(quarters, im_send.at[0]))
+    pl.when(c == 0)(lambda: sent(quarters, im_send.at[1]))
+    pl.when(c == 1)(lambda: sent(im_all.at[0, :, :, 0, 0], im_send.at[2]))
+    pl.when(ahead)(lambda: sent(u_all.at[0, first_pair], u_send.at[3]))
+    pl.when(ahead)(lambda: sent(im_all.at[0, :, :, 0], im_send.at[3]))
+    pl.when(jnp.logical_not(ahead))(lambda: sent(u_all.at[0, first_pair], u_send.at[4]))
+    pl.when(jnp.logical_not(ahead))(lambda: sent(im_all.at[0, :, :, 0, 0], im_send.at[4]))
+
+
+def combine(u_all, im_all, rows_ref, ortho_hbm, renew_hbm, r_ref, ortho, renew, coef_ref, out_sem):
+    c = lax.axis_index("col")
+    row16 = lax.broadcasted_iota(jnp.int32, (16, 128), 0)
+    lane16 = lax.broadcasted_iota(jnp.int32, (16, 128), 1)
+    r_ref[...] = jnp.where(lane16 >= row16, rows_ref[...], 0.0)[:, :16]
     own = rows_ref[pl.ds(4 * c, 4), :]
     for i in range(4):
         for j in range(16):
-            coef_ref[i, j] = jnp.broadcast_to(own[i : i + 1, 16 + j : 17 + j], (8, 256))
-
-    for copy in ag_copies:
-        copy.wait()
-
-    def combine(step, carry):
+            coef_ref[i, j] = jnp.broadcast_to(own[i : i + 1, 16 + j : 17 + j], (8, 128))
+
+    def used(j, value):
+        return value if j < 4 else jnp.where(j // 4 <= c, value, 0.0)
+
+    def outputs(step):
         a, l = step // 2, step % 2
-        for source, target in ((u_all, renew_ref), (im_all, ortho_ref)):
-            acc = [None] * 4
-            for j in range(16):
-                value = source[j // 4, j % 4, a, l]
+        return [
+            pltpu.make_async_copy(ortho.at[:, a, l], ortho_hbm.at[:, a, l], out_sem.at[0]),
+            pltpu.make_async_copy(renew.at[:, a, l], renew_hbm.at[:, a, l], out_sem.at[1]),
+        ]
+
+    def one(step, carry):
+        a, l = step // 2, step % 2
+        for h in range(2):
+            for source, target in ((u_all, renew), (im_all, ortho)):
+                acc = [None] * 4
+                for j in range(16):
+                    if source is u_all:
+                        value = source[j // 4, j % 4, a, l, :, 128 * h : 128 * h + 128]
+                    else:
+                        value = source[j // 4, j % 4, a, l, h]
+                    value = used(j, value)
+                    for i in range(4):
+                        term = coef_ref[i, j] * value
+                        acc[i] = term if acc[i] is None else acc[i] + term
                 for i in range(4):
-                    term = coef_ref[i, j] * value
-                    acc[i] = term if acc[i] is None else acc[i] + term
-            for i in range(4):
-                target[i, a, l] = acc[i]
+                    target[i, a, l, :, 128 * h : 128 * h + 128] = acc[i]
+        for copy in outputs(step):
+            copy.start()
         return carry
 
-    lax.fori_loop(0, 6, combine, 0)
+    lax.fori_loop(0, 6, one, 0)
+    pltpu.make_async_copy(ortho, ortho_hbm, out_sem.at[0]).wait()
+    pltpu.make_async_copy(renew, renew_hbm, out_sem.at[1]).wait()
 
 
 def solution(mesh):
@@ -367,33 +454,46 @@
         hbm = pl.BlockSpec(memory_space=pl.ANY)
         dma = pltpu.SemaphoreType.DMA
         layer = shape[3:]
+        u_all, im_all, rows = pl.pallas_call(
+            functools.partial(exchange, slabs, cols, constants, float(rows_total)),
+            out_shape=(
+                pltpu.VMEM((cols,) + shape, f32),
+                pltpu.VMEM((cols,) + shape[:3] + (2, 8, 128), f32),
+                pltpu.VMEM((16, 128), f32),
+            ),
+            in_specs=[hbm] * 4,
+            out_specs=(vmem, vmem, vmem),
+            scratch_shapes=[
+                pltpu.VMEM((2, 4, 3) + layer, f32),
+                pltpu.VMEM((3,) + layer, f32),
+                pltpu.VMEM((3,) + layer, jnp.int32),
+                pltpu.VMEM((4,) + layer, jnp.int32),
+                pltpu.VMEM((3, len(constants)) + layer, f32),
+                pltpu.VMEM((cols * 8, 2, 128), f32),
+                pltpu.VMEM((slabs // 8, 2, 128), f32),
+                dma((4,)), dma((5,)), dma((5,)), dma((5,)), dma((5,)),
+                dma, dma, dma((5,)), dma((5,)), dma((2,)), dma((2,)),
+                pltpu.SemaphoreType.REGULAR, pltpu.SemaphoreType.REGULAR((2,)),
+            ],
+            compiler_params=pltpu.CompilerParams(collective_id=0, has_side_effects=True),
+        )(recycle_basis, densities, solid_mask, fixed_mask)
+        kept = [pltpu.with_memory_space_constraint(x, pltpu.VMEM) for x in (u_all, im_all, rows)]
         return pl.pallas_call(
-            functools.partial(body, slabs, cols, constants, float(rows_total)),
+            combine,
             out_shape=(
                 jax.ShapeDtypeStruct(shape, f32),
                 jax.ShapeDtypeStruct(shape, f32),
                 jax.ShapeDtypeStruct((16, 16), f32),
             ),
-            in_specs=[hbm] * 4,
-            out_specs=(vmem, vmem, vmem),
+            in_specs=[vmem] * 3,
+            out_specs=(hbm, hbm, vmem),
             scratch_shapes=[
-                pltpu.VMEM((cols,) + shape, f32),
-                pltpu.VMEM((cols,) + shape, f32),
-                pltpu.VMEM((2, 4, 3) + layer, f32),
-                pltpu.VMEM((3,) + layer, f32),
-                pltpu.VMEM((3,) + layer, jnp.int32),
-                pltpu.VMEM((4,) + layer, jnp.int32),
-                pltpu.VMEM((3, len(constants)) + layer, f32),
-                pltpu.VMEM((8, 16, 128), f32),
-                pltpu.VMEM((8, 16, 128), f32),
-                pltpu.VMEM((16, 128), f32),
-                pltpu.VMEM((4, 16, 8, 256), f32),
-                dma((4,)), dma((6,)), dma((6,)),
-                dma((4,)), dma((4,)), dma((4,)), dma((4,)),
-                dma((8,)), dma((8,)), dma((8,)), dma((8,)),
+                pltpu.VMEM(shape, f32),
+                pltpu.VMEM(shape, f32),
+                pltpu.VMEM((4, 16, 8, 128), f32),
+                dma((2,)),
             ],
-            compiler_params=pltpu.CompilerParams(collective_id=0, has_side_effects=True),
-        )(recycle_basis, densities, solid_mask, fixed_mask)
+        )(*kept)
 
     placed = (
         P("col", None, "slab", None, None),

time: 41.4 us -> 32.1 us (0.78)
  Pallas kernels: 37.7 us -> 31.4 us
  local copies, waits for them, and re-layouts: 2.95 us -> 0 us
    pallas_call x1 -> x2, Pallas kernels: 37.7 us -> 31.4 us  [the longest x1 29.4 us: on_device(): pl.pallas_call(functools.partial(exchange, slabs, cols, constants, float(...]
    unnamed x7 -> x0, local copies, waits for them, and re-layouts: 2.95 us -> none
where the time goes in v2:
time: 32.1 us; the launch traced here: 32 us
  Pallas kernels  31.4 us (98%)
  between operations  0.64 us (2%)
    pallas_call x1, Pallas kernels, on_device(): pl.pallas_call(functools.partial(exchange, slabs, cols, constants, float(...  29.4 us
    pallas_call x1, Pallas kernels, on_device(): pl.pallas_call(combine, out_shape=(jax.ShapeDtypeStruct(shape, f32), jax....  1.92 us

profile of v2, /device:TPU:1, one launch (start us, length us, event | category | flops | bytes accessed | tf_op | source)
XLA Modules:
  0.0 32.0 jit_solution(13029488351394738037)
XLA Ops:
  0.6 29.4 %shard_map.67 = (f32[4,4,3,2,8,256]{5,4,3,2,1,0:T(8,128)S(1)}, f32[4,4,3,2,2,8,128]{6,5,4,3,2,1,0:T(8,128)S(1)}, f32[16,128]{1,0:T(8,128)S(1)}) custom-call(f32[4,3,2,8,256]{4,3,2,1,0:T(8,128)} %u_hbm.1, f32[2,8,256]{2,1,0:T(8,128)} %dens_hbm.1, s32[2,8,256]{2,1,0:T(8,128)} %solid_hbm.1, s32[2,8,256]{2,1,0:T(8,128)} %fixed_hbm.1), custom_call_target="tpu_custom_call" | custom-call | tf_op jit(solution)/shard_map/pallas_call | solution.py:457
  30.1 1.9 %shard_map.68 = (f32[4,3,2,8,256]{4,3,2,1,0:T(8,128)}, f32[4,3,2,8,256]{4,3,2,1,0:T(8,128)}, f32[16,16]{1,0:T(8,128)}) custom-call(f32[4,4,3,2,8,256]{5,4,3,2,1,0:T(8,128)S(1)} %get-tuple-element.6.u_all, f32[4,4,3,2,2,8,128]{6,5,4,3,2,1,0:T(8,128)S(1)} %get-tuple-element.7.im_all, f32[16,128]{1,0:T(8,128)S(1)} %get-tuple-element.8.rows_ref), custom_call_target="tpu_custom_call" | custom-call | tf_op jit(solution)/shard_map/pallas_call | solution.py:481

commit v3 on v2

--- a/solution.py
+++ b/solution.py
@@ -235,12 +235,12 @@
         remote(u_hbm.at[j, :, 0], halo.at[1, j], halo_send.at[j], halo_recv.at[j], down).start()
 
     first_pair, last_pair = (pl.ds(0, 2), pl.ds(2, 2))
-    u_next = remote(u_hbm, u_all.at[c], u_send.at[0], u_recv.at[0], along_x(1))
-    u_wrap = remote(u_hbm, u_all.at[c], u_send.at[1], u_recv.at[1], along_x(-1))
-    u_back = remote(u_hbm.at[last_pair], u_all.at[c, last_pair], u_send.at[2], u_recv.at[2], along_x(-1))
-    pl.when(c < cols - 1)(u_next.start)
-    pl.when(c == 0)(u_wrap.start)
-    pl.when(c == 1)(u_back.start)
+    def share(part):
+        ref = u_all.at[c, part]
+        pl.when(c < cols - 1)(remote(u_hbm.at[part], ref, u_send.at[0], u_recv.at[0], along_x(1)).start)
+        pl.when(c == 0)(remote(u_hbm.at[part], ref, u_send.at[1], u_recv.at[1], along_x(-1)).start)
+
+    share(pl.ds(0, 3))
 
     for k in range(1, cols):
         pl.semaphore_signal(ready_x, inc=1, device_id=along_x(k), device_id_type=MESH)
@@ -280,13 +280,17 @@
                 value = free[l + 1] * out[l, a] + (1.0 - free[l + 1]) * raw[l][a]
                 im_all[c, j, a, l, 0] = value[:, :128]
                 im_all[c, j, a, l, 1] = value[:, 128:]
-        for k in range(1, cols):
+        for k in (2, 1, 3):
             t = lax.rem(c + k, cols)
             piece = im_all.at[c, j, :, t // 2, t % 2]
             remote(piece, piece, q_send, q_recv, at(s, t)).start()
         return carry
 
     lax.fori_loop(0, 4, one_column, 0)
+
+    share(pl.ds(3, 1))
+    u_back = remote(u_hbm.at[last_pair], u_all.at[c, last_pair], u_send.at[2], u_recv.at[2], along_x(-1))
+    pl.when(c == 1)(u_back.start)
 
     pl.semaphore_wait(ready_z.at[0], 2)
     for k in (2, -2):
@@ -317,11 +321,10 @@
 
     slot = c * group + yc
     gram_a[slot] = packed
-    for k in range(1, wide):
-        other = lax.rem(slot + k, wide)
-        remote(
-            gram_a.at[slot], gram_a.at[slot], gram_send.at[0], gram_recv.at[0], at(zi * group + other % group, other // group)
-        ).start()
+    hops = [(min(k, cols - k) + min(m // 2, group // 2 - m // 2), k, m) for k in range(cols) for m in range(group)]
+    for _, k, m in sorted(hops, reverse=True)[:-1]:
+        where = at(zi * group + lax.rem(yc + m, group), lax.rem(c + k, cols))
+        remote(gram_a.at[slot], gram_a.at[slot], gram_send.at[0], gram_recv.at[0], where).start()
 
     for k in range(1, cols):
         t = lax.rem(c + 1 + k, cols)
@@ -347,7 +350,7 @@
     summed = jnp.sum(gram_a[...], axis=0)
     gram_b[zi] = summed
     pl.semaphore_wait(ready_z.at[1], 2)
-    for k in range(1, zn):
+    for k in sorted(range(1, zn), key=lambda k: -min(k, zn - k)):
         remote(gram_b.at[zi], gram_b.at[zi], gram_send.at[1], gram_recv.at[1], along_z(k)).start()
 
     pl.when(c >= 1)(lambda: received(quarters, im_recv.at[0]))
@@ -367,14 +370,30 @@
     gram = exact_dot(kept, picked) * (1.0 / rows_total)
 
     work = jnp.where(lane16 < 16, gram, (lane16 == row16 + 16).astype(f32))
-    for k in range(16):
-        pivot = work[k : k + 1, k : k + 1]
-        scale = lax.rsqrt(pivot)
-        scale = scale * (1.5 - 0.5 * pivot * scale * scale)
-        row = work[k : k + 1, :] * scale
-        rows_ref[k : k + 1, :] = row
-        if k < 15:
-            work = work - (work[:, k : k + 1] * scale) * row
+    for first in range(0, 16, 4):
+        ids = range(4)
+        side = [jnp.broadcast_to(work[:, first + b : first + b + 1], (16, 128)) for b in ids]
+        rows = [work[first + a : first + a + 1] for a in ids]
+        low = {}
+        scale = []
+        for b in ids:
+            for a in range(b, 4):
+                value = side[b][first + a : first + a + 1]
+                for d in range(b):
+                    value = value - low[a, d] * low[b, d]
+                if a == b:
+                    scale.append(lax.rsqrt(value))
+                else:
+                    low[a, b] = value * scale[b]
+        for b in ids:
+            for d in range(b):
+                rows[b] = rows[b] - low[b, d] * rows[d]
+                side[b] = side[b] - side[d] * low[b, d]
+            rows[b] = rows[b] * scale[b]
+            side[b] = side[b] * scale[b]
+            rows_ref[first + b : first + b + 1, :] = rows[b]
+        if first < 12:
+            work = work - ((side[0] * rows[0] + side[1] * rows[1]) + (side[2] * rows[2] + side[3] * rows[3]))
 
     pl.when((c == 2) | (c == 3))(lambda: received(u_all.at[0, first_pair], u_recv.at[3]))
     pl.when((c == 2) | (c == 3))(lambda: received(u_all.at[0, first_pair], u_recv.at[4]))

time: 32.1 us -> 29.5 us (0.919)
  Pallas kernels: 31.4 us -> 28.8 us
    pallas_call x1, Pallas kernels: 29.4 us -> 26.9 us  [on_device(): pl.pallas_call(functools.partial(exchange, slabs, cols, constants, float(...]
where the time goes in v3:
time: 29.5 us; the launch traced here: 29.4 us
  Pallas kernels  28.8 us (98%)
  between operations  0.64 us (2%)
    pallas_call x1, Pallas kernels, on_device(): pl.pallas_call(functools.partial(exchange, slabs, cols, constants, float(...  26.9 us
    pallas_call x1, Pallas kernels, on_device(): pl.pallas_call(combine, out_shape=(jax.ShapeDtypeStruct(shape, f32), jax....  1.92 us

profile of v3, /device:TPU:1, one launch (start us, length us, event | category | flops | bytes accessed | tf_op | source)
XLA Modules:
  0.0 29.4 jit_solution(9507710055164068086)
XLA Ops:
  0.6 26.9 %shard_map.67 = (f32[4,4,3,2,8,256]{5,4,3,2,1,0:T(8,128)S(1)}, f32[4,4,3,2,2,8,128]{6,5,4,3,2,1,0:T(8,128)S(1)}, f32[16,128]{1,0:T(8,128)S(1)}) custom-call(f32[4,3,2,8,256]{4,3,2,1,0:T(8,128)} %u_hbm.1, f32[2,8,256]{2,1,0:T(8,128)} %dens_hbm.1, s32[2,8,256]{2,1,0:T(8,128)} %solid_hbm.1, s32[2,8,256]{2,1,0:T(8,128)} %fixed_hbm.1), custom_call_target="tpu_custom_call" | custom-call | tf_op jit(solution)/shard_map/pallas_call | solution.py:476
  27.5 1.9 %shard_map.68 = (f32[4,3,2,8,256]{4,3,2,1,0:T(8,128)}, f32[4,3,2,8,256]{4,3,2,1,0:T(8,128)}, f32[16,16]{1,0:T(8,128)}) custom-call(f32[4,4,3,2,8,256]{5,4,3,2,1,0:T(8,128)S(1)} %get-tuple-element.6.u_all, f32[4,4,3,2,2,8,128]{6,5,4,3,2,1,0:T(8,128)S(1)} %get-tuple-element.7.im_all, f32[16,128]{1,0:T(8,128)S(1)} %get-tuple-element.8.rows_ref), custom_call_target="tpu_custom_call" | custom-call | tf_op jit(solution)/shard_map/pallas_call | solution.py:500

commit v4 on v3

--- a/solution.py
+++ b/solution.py
@@ -182,24 +182,30 @@
 ):
     s = lax.axis_index("slab")
     c = lax.axis_index("col")
-    group = 8
-    zi, yc = s // group, s % group
-    zn = slabs // group
-    wide = cols * group
+    zn = slabs // 8
+    zi = lax.div(s, 8)
+    yc = s - 8 * zi
+    yi = lax.div(yc, 2)
+    core = yc - 2 * yi
+    plane, depth2 = (cols * 8, zn)
+
+    def wrap(value, k, count):
+        moved = value + k % count
+        return jnp.where(moved >= count, moved - count, moved)
 
     def at(slab, col):
         return {"slab": slab, "col": col}
 
     def along_x(k):
-        return at(s, lax.rem(c + k + cols, cols))
-
-    def along_z(k):
-        return at(lax.rem(zi + k + zn, zn) * group + yc, c)
-
-    up, down = (at(lax.rem(s + 1, slabs), c), at(lax.rem(s + slabs - 1, slabs), c))
-    near = [up, down, along_z(1), along_z(-1)]
+        return at(s, wrap(c, k, cols))
+
+    def along_z(k, m=0):
+        return at(wrap(zi, k, zn) * 8 + 2 * yi + (1 - core if m else core), c)
+
+    up, down = (at(wrap(s, 1, slabs), c), at(wrap(s, -1, slabs), c))
+    near = [up, down] + [along_z(k) for k in (1, -1)]
     near += [along_x(k) for k in range(1, cols)]
-    near += [at(zi * group + lax.rem(yc + k, group), c) for k in range(1, group)]
+    near += [at(8 * zi + wrap(yc, k, 8), c) for k in range(1, 8)]
 
     local = [
         pltpu.make_async_copy(u_hbm, u_all.at[c], local_sem.at[0]),
@@ -212,6 +218,8 @@
         pl.semaphore_signal(barrier, inc=1, device_id=partner, device_id_type=MESH)
     for copy in local:
         copy.start()
+    for copy in local:
+        copy.wait()
     pl.semaphore_wait(barrier, len(near))
 
     def remote(src, dst, send, recv, where):
@@ -226,19 +234,19 @@
         remote(ref, ref, sem, sem, along_x(1)).wait_send()
 
     small_send, small_recv = (halo_send.at[4], halo_recv.at[4])
-    remote(dens_hbm.at[1], dens.at[0], small_send, small_recv, up).start()
-    remote(solid_hbm.at[1], solid.at[0], small_send, small_recv, up).start()
-    remote(fixed_hbm.at[1], fixed.at[0], small_send, small_recv, up).start()
-    remote(fixed_hbm.at[0], fixed.at[3], small_send, small_recv, down).start()
+    remote(dens.at[2], dens.at[0], small_send, small_recv, up).start()
+    remote(solid.at[2], solid.at[0], small_send, small_recv, up).start()
+    remote(fixed.at[2], fixed.at[0], small_send, small_recv, up).start()
+    remote(fixed.at[1], fixed.at[3], small_send, small_recv, down).start()
     for j in range(4):
-        remote(u_hbm.at[j, :, 1], halo.at[0, j], halo_send.at[j], halo_recv.at[j], up).start()
-        remote(u_hbm.at[j, :, 0], halo.at[1, j], halo_send.at[j], halo_recv.at[j], down).start()
+        remote(u_all.at[c, j, :, 1], halo.at[0, j], halo_send.at[j], halo_recv.at[j], up).start()
+        remote(u_all.at[c, j, :, 0], halo.at[1, j], halo_send.at[j], halo_recv.at[j], down).start()
 
     first_pair, last_pair = (pl.ds(0, 2), pl.ds(2, 2))
     def share(part):
         ref = u_all.at[c, part]
-        pl.when(c < cols - 1)(remote(u_hbm.at[part], ref, u_send.at[0], u_recv.at[0], along_x(1)).start)
-        pl.when(c == 0)(remote(u_hbm.at[part], ref, u_send.at[1], u_recv.at[1], along_x(-1)).start)
+        pl.when(c < cols - 1)(remote(ref, ref, u_send.at[0], u_recv.at[0], along_x(1)).start)
+        pl.when(c == 0)(remote(ref, ref, u_send.at[1], u_recv.at[1], along_x(-1)).start)
 
     share(pl.ds(0, 3))
 
@@ -247,8 +255,6 @@
     for k in (1, -1):
         pl.semaphore_signal(ready_z.at[0], inc=1, device_id=along_z(k), device_id_type=MESH)
 
-    for copy in local:
-        copy.wait()
     received(fixed, small_recv)
 
     node = lax.broadcasted_iota(jnp.int32, (8, 256), 0)
@@ -263,6 +269,10 @@
             scaled[e, k] = value * constant
 
     lane = lax.broadcasted_iota(jnp.int32, (8, 128), 1)
+
+    def halves(t):
+        layer = jnp.where(t >= 2, 1, 0)
+        return (layer, t - 2 * layer)
 
     def one_column(j, carry):
         free = [1.0 - fixed[l].astype(f32) for l in range(4)]
@@ -281,15 +291,15 @@
                 im_all[c, j, a, l, 0] = value[:, :128]
                 im_all[c, j, a, l, 1] = value[:, 128:]
         for k in (2, 1, 3):
-            t = lax.rem(c + k, cols)
-            piece = im_all.at[c, j, :, t // 2, t % 2]
+            t = wrap(c, k, cols)
+            piece = im_all.at[c, j, :, *halves(t)]
             remote(piece, piece, q_send, q_recv, at(s, t)).start()
         return carry
 
     lax.fori_loop(0, 4, one_column, 0)
 
     share(pl.ds(3, 1))
-    u_back = remote(u_hbm.at[last_pair], u_all.at[c, last_pair], u_send.at[2], u_recv.at[2], along_x(-1))
+    u_back = remote(u_all.at[c, last_pair], u_all.at[c, last_pair], u_send.at[2], u_recv.at[2], along_x(-1))
     pl.when(c == 1)(u_back.start)
 
     pl.semaphore_wait(ready_z.at[0], 2)
@@ -300,7 +310,7 @@
     quarters = im_all.at[pl.ds(0, cols - 1), :, :, 0, 0]
     received(quarters, q_recv)
 
-    mine_l, mine_h = (c // 2, c % 2)
+    mine_l, mine_h = halves(c)
     sides = []
     for a in range(3):
         block = im_all[:, :, a, mine_l, mine_h].reshape(128, 128)
@@ -319,16 +329,15 @@
     pairs = exact_dot(pairs, spread)
     packed = jnp.where(row16 % 8 == lane16 % 8, pairs, 0.0).reshape(2, 8, 128).sum(axis=1)
 
-    slot = c * group + yc
+    slot = 8 * c + yc
     gram_a[slot] = packed
-    hops = [(min(k, cols - k) + min(m // 2, group // 2 - m // 2), k, m) for k in range(cols) for m in range(group)]
+    hops = [(min(k, cols - k) + min(m // 2, 4 - m // 2), k, m) for k in range(cols) for m in range(8)]
     for _, k, m in sorted(hops, reverse=True)[:-1]:
-        where = at(zi * group + lax.rem(yc + m, group), lax.rem(c + k, cols))
+        where = at(8 * zi + wrap(yc, m, 8), wrap(c, k, cols))
         remote(gram_a.at[slot], gram_a.at[slot], gram_send.at[0], gram_recv.at[0], where).start()
 
     for k in range(1, cols):
-        t = lax.rem(c + 1 + k, cols)
-        piece = im_all.at[c, :, :, t // 2, t % 2]
+        piece = im_all.at[c, :, :, *halves(wrap(c, 1 + k, cols))]
         pl.when(c < cols - 1)(remote(piece, piece, im_send.at[0], im_recv.at[0], along_x(1)).start)
         piece = im_all.at[c, :, :, (k - 1) // 2, (k - 1) % 2]
         pl.when(c == 0)(remote(piece, piece, im_send.at[1], im_recv.at[1], along_x(-1)).start)
@@ -337,7 +346,7 @@
     pl.when(c == 1)(im_back.start)
 
     ahead = (c == 1) | (c == 2)
-    relay_block = jnp.where(ahead, c - 1, lax.rem(c + 1, cols))
+    relay_block = jnp.where(ahead, c - 1, wrap(c, 1, cols))
     pl.when(c >= 1)(lambda: received(u_all.at[0], u_recv.at[0]))
     pl.when(c == 3)(lambda: received(u_all.at[0], u_recv.at[1]))
     pl.when(c == 0)(lambda: received(u_all.at[0, last_pair], u_recv.at[2]))
@@ -346,10 +355,9 @@
     ref = u_all.at[relay_block, last_pair]
     pl.when(jnp.logical_not(ahead))(remote(ref, ref, u_send.at[4], u_recv.at[4], along_x(-1)).start)
 
-    received(gram_a.at[pl.ds(0, wide - 1)], gram_recv.at[0])
-    summed = jnp.sum(gram_a[...], axis=0)
-    gram_b[zi] = summed
     pl.semaphore_wait(ready_z.at[1], 2)
+    received(gram_a.at[pl.ds(0, plane - 1)], gram_recv.at[0])
+    gram_b[zi] = jnp.sum(gram_a[...], axis=0)
     for k in sorted(range(1, zn), key=lambda k: -min(k, zn - k)):
         remote(gram_b.at[zi], gram_b.at[zi], gram_send.at[1], gram_recv.at[1], along_z(k)).start()
 
@@ -361,7 +369,7 @@
     ref = im_all.at[relay_block, :, :, 1, jnp.where(c == 3, 1, 0)]
     pl.when(jnp.logical_not(ahead))(remote(ref, ref, im_send.at[4], im_recv.at[4], along_x(-1)).start)
 
-    received(gram_b.at[pl.ds(0, zn - 1)], gram_recv.at[1])
+    received(gram_b.at[pl.ds(0, depth2 - 1)], gram_recv.at[1])
     summed = jnp.sum(gram_b[...], axis=0)
 
     wide_rows = jnp.concatenate([jnp.broadcast_to(summed[r : r + 1], (8, 128)) for r in range(2)], axis=0)
@@ -403,8 +411,8 @@
     for j in range(4):
         sent(halo.at[:, 0], halo_send.at[j])
     sent(quarters, q_send)
-    sent(gram_a.at[pl.ds(0, wide - 1)], gram_send.at[0])
-    sent(gram_b.at[pl.ds(0, zn - 1)], gram_send.at[1])
+    sent(gram_a.at[pl.ds(0, plane - 1)], gram_send.at[0])
+    sent(gram_b.at[pl.ds(0, depth2 - 1)], gram_send.at[1])
     pl.when(c < cols - 1)(lambda: sent(u_all.at[0], u_send.at[0]))
     pl.when(c == 0)(lambda: sent(u_all.at[0], u_send.at[1]))
     pl.when(c == 1)(lambda: sent(u_all.at[0, first_pair], u_send.at[2]))
@@ -417,15 +425,15 @@
     pl.when(jnp.logical_not(ahead))(lambda: sent(im_all.at[0, :, :, 0, 0], im_send.at[4]))
 
 
-def combine(u_all, im_all, rows_ref, ortho_hbm, renew_hbm, r_ref, ortho, renew, coef_ref, out_sem):
+def combine(u_all, im_all, rows_ref, ortho_hbm, renew_hbm, r_hbm, ortho, renew, r_ref, coef_ref, out_sem):
     c = lax.axis_index("col")
     row16 = lax.broadcasted_iota(jnp.int32, (16, 128), 0)
     lane16 = lax.broadcasted_iota(jnp.int32, (16, 128), 1)
     r_ref[...] = jnp.where(lane16 >= row16, rows_ref[...], 0.0)[:, :16]
+    factor_out = pltpu.make_async_copy(r_ref, r_hbm, out_sem.at[2])
     own = rows_ref[pl.ds(4 * c, 4), :]
-    for i in range(4):
-        for j in range(16):
-            coef_ref[i, j] = jnp.broadcast_to(own[i : i + 1, 16 + j : 17 + j], (8, 128))
+    for j in range(16):
+        coef_ref[j] = jnp.broadcast_to(own[:, 16 + j : 17 + j], (4, 128))
 
     def used(j, value):
         return value if j < 4 else jnp.where(j // 4 <= c, value, 0.0)
@@ -449,7 +457,7 @@
                         value = source[j // 4, j % 4, a, l, h]
                     value = used(j, value)
                     for i in range(4):
-                        term = coef_ref[i, j] * value
+                        term = coef_ref[j, i : i + 1, :] * value
                         acc[i] = term if acc[i] is None else acc[i] + term
                 for i in range(4):
                     target[i, a, l, :, 128 * h : 128 * h + 128] = acc[i]
@@ -457,9 +465,11 @@
             copy.start()
         return carry
 
+    factor_out.start()
     lax.fori_loop(0, 6, one, 0)
     pltpu.make_async_copy(ortho, ortho_hbm, out_sem.at[0]).wait()
     pltpu.make_async_copy(renew, renew_hbm, out_sem.at[1]).wait()
+    factor_out.wait()
 
 
 def solution(mesh):
@@ -505,12 +515,13 @@
                 jax.ShapeDtypeStruct((16, 16), f32),
             ),
             in_specs=[vmem] * 3,
-            out_specs=(hbm, hbm, vmem),
+            out_specs=(hbm, hbm, hbm),
             scratch_shapes=[
                 pltpu.VMEM(shape, f32),
                 pltpu.VMEM(shape, f32),
-                pltpu.VMEM((4, 16, 8, 128), f32),
-                dma((2,)),
+                pltpu.VMEM((16, 16), f32),
+                pltpu.VMEM((16, 4, 128), f32),
+                dma((3,)),
             ],
         )(*kept)
 

time: 29.5 us -> 28.7 us (0.973)
  Pallas kernels: 28.8 us -> 27.9 us
    pallas_call x1, Pallas kernels: 1.92 us -> 1.25 us  [on_device(): pl.pallas_call(combine, out_shape=(jax.ShapeDtypeStruct(shape, f32), jax....]
where the time goes in v4:
time: 28.7 us; the launch traced here: 28.6 us
  Pallas kernels  27.9 us (97%)
  between operations  0.64 us (2%)
    pallas_call x1, Pallas kernels, on_device(): pl.pallas_call(functools.partial(exchange, slabs, cols, constants, float(...  26.7 us
    pallas_call x1, Pallas kernels, on_device(): pl.pallas_call(combine, out_shape=(jax.ShapeDtypeStruct(shape, f32), jax....  1.25 us

profile of v4, /device:TPU:1, one launch (start us, length us, event | category | flops | bytes accessed | tf_op | source)
XLA Modules:
  0.0 28.6 jit_solution(5060186918142350940)
XLA Ops:
  0.6 26.7 %shard_map.67 = (f32[4,4,3,2,8,256]{5,4,3,2,1,0:T(8,128)S(1)}, f32[4,4,3,2,2,8,128]{6,5,4,3,2,1,0:T(8,128)S(1)}, f32[16,128]{1,0:T(8,128)S(1)}) custom-call(f32[4,3,2,8,256]{4,3,2,1,0:T(8,128)} %u_hbm.1, f32[2,8,256]{2,1,0:T(8,128)} %dens_hbm.1, s32[2,8,256]{2,1,0:T(8,128)} %solid_hbm.1, s32[2,8,256]{2,1,0:T(8,128)} %fixed_hbm.1), custom_call_target="tpu_custom_call" | custom-call | tf_op jit(solution)/shard_map/pallas_call | solution.py:486
  27.3 1.3 %shard_map.68 = (f32[4,3,2,8,256]{4,3,2,1,0:T(8,128)}, f32[4,3,2,8,256]{4,3,2,1,0:T(8,128)}, f32[16,16]{1,0:T(8,128)}) custom-call(f32[4,4,3,2,8,256]{5,4,3,2,1,0:T(8,128)S(1)} %get-tuple-element.6.u_all, f32[4,4,3,2,2,8,128]{6,5,4,3,2,1,0:T(8,128)S(1)} %get-tuple-element.7.im_all, f32[16,128]{1,0:T(8,128)S(1)} %get-tuple-element.8.rows_ref), custom_call_target="tpu_custom_call" | custom-call | tf_op jit(solution)/shard_map/pallas_call | solution.py:510
